TPU v7x, 32 devices: a whole 2x2x4 slice. The times are simulated.
32 devices in a mesh: chan: 4 (over y, x), hid: 8 (over z, core).
Axes of the slice: x: 2, y: 2, z: 4, core: 2. Of those that a mesh axis runs over, the one named last changes fastest.
Arguments:
- pixels: bfloat16 [384, 256, 256], P('chan'), may hold values from -6 to 6
- patch_weight: bfloat16 [384, 256, 6144], P('chan', None, 'hid'), may hold values from -0.375 to 0.375
- channel_embed: bfloat16 [384, 6144], P('chan', 'hid'), may hold values from -3 to 3
- pool_query: bfloat16 [48, 6144], P('chan', 'hid'), may hold values from -2.5 to 2.5
- group_mix: bfloat16 [48, 6144], P('chan', 'hid'), may hold values from -3.2 to 3.2
- assign: int32 [384], P('chan'), may hold values from 0 to 47, as said below
- ln_gain: float32 [6144], P('chan'), may hold values from 0.1 to 1.9
- w_qkv: bfloat16 [6144, 3, 6144], P('chan', None, 'hid'), may hold values from -0.078125 to 0.078125
- w_up: bfloat16 [6144, 24576], P('chan', 'hid'), may hold values from -0.078125 to 0.078125
- b_up: float32 [24576], P('hid'), may hold values from -3 to 3
- w_out: bfloat16 [6144, 6144], P('hid', 'chan'), may hold values from -0.078125 to 0.078125
- w_down: bfloat16 [24576, 6144], P('hid', 'chan'), may hold values from -0.0390625 to 0.0390625
Outputs:
- block_out: bfloat16 [256, 6144], P(None, 'chan')
Inputs may be any that keep to these rules, and one draw needn't show every extreme that they name: Channel c belongs to group assign[c]; every group holds exactly 8 channels, and group k's channels all lie among the 96 consecutive channels beginning at channel (k // 12) * 96.
All inputs are finite; a program needn't handle non-finite values.
Results may differ from a plain program's by a relative error of at most 0.02.
Values may be sent and summed in bfloat16 or wider, within the bound.
A program may use at most 320 MiB of HBM per device.

v0:
```python
import math

import jax
import jax.numpy as jnp
from jax import lax
from jax.sharding import PartitionSpec as P

HS = 128
PATCHES = 256
D = 6144


epsilon = 1e-06


def head_norm(values):
    return values * lax.rsqrt(jnp.mean(values * values, axis=-1, keepdims=True) + epsilon)


def finish_rows(qkv_rows, up_rows, b_up, heads_dev):
    rows = qkv_rows.shape[0]
    width = heads_dev * HS
    query_part = (
        head_norm(qkv_rows[:, 0].reshape(rows, heads_dev, HS))
        .astype(jnp.bfloat16)
        .reshape(rows, width)
    )
    key_part = (
        head_norm(qkv_rows[:, 1].reshape(rows, heads_dev, HS))
        .astype(jnp.bfloat16)
        .reshape(rows, width)
    )
    value_part = qkv_rows[:, 2].astype(jnp.bfloat16)
    hidden_part = jax.nn.gelu(up_rows + b_up, approximate=False).astype(jnp.bfloat16)
    return (query_part, key_part, value_part, hidden_part)


def on_device(
    pixels,
    patch_weight,
    channel_embed,
    pool_query,
    group_mix,
    assign,
    ln_gain,
    w_qkv,
    w_up,
    b_up,
    w_out,
    w_down,
):
    chan_count = pixels.shape[0]
    tok_count = pixels.shape[1]
    width_hid = patch_weight.shape[2]
    width_chan = ln_gain.shape[0]
    heads_dev = width_hid // HS
    groups_dev = pool_query.shape[0]
    embedded = jnp.einsum("ctp,cpd->ctd", pixels, patch_weight, preferred_element_type=jnp.float32)
    embedded = embedded + channel_embed.astype(jnp.float32)[:, None, :]
    features = jax.nn.gelu(embedded, approximate=False)
    split = features.reshape(chan_count, tok_count, heads_dev, HS)
    normed = head_norm(split)
    local_group = assign - lax.axis_index("chan") * groups_dev
    member = (local_group[None, :] == jnp.arange(groups_dev, dtype=jnp.int32)[:, None]).astype(
        jnp.float32
    )
    query = jnp.dot(member.T, pool_query.astype(jnp.float32), precision=lax.Precision.HIGHEST)
    query = query.reshape(chan_count, heads_dev, HS)
    score = jnp.einsum("cthe,che->cth", normed, query, precision=lax.Precision.HIGHEST) / math.sqrt(
        HS
    )
    shift = jnp.sqrt(jnp.sum(query * query, axis=-1))
    weight = jnp.exp(score - shift[:, None, :])
    numer = jnp.einsum(
        "kc,cthe->kthe", member, weight[..., None] * split, precision=lax.Precision.HIGHEST
    )
    denom = jnp.einsum("kc,cth->kth", member, weight, precision=lax.Precision.HIGHEST)
    pooled = (numer / denom[..., None]).reshape(groups_dev, tok_count, width_hid)
    partial_value = jnp.einsum(
        "kd,ktd->td", group_mix.astype(jnp.float32), pooled, precision=lax.Precision.HIGHEST
    )
    layer_sum = lax.psum(partial_value.astype(jnp.bfloat16), "chan")
    gathered = lax.all_gather(layer_sum, "hid", axis=1, tiled=True)
    wide = gathered.astype(jnp.float32)
    row_total = jnp.sum(wide, axis=1)
    row_square = jnp.sum(wide * wide, axis=1)
    mine = lax.dynamic_slice_in_dim(gathered, lax.axis_index("chan") * width_chan, width_chan, 1)
    row_mean = row_total / D
    row_var = row_square / D - row_mean * row_mean
    own_cols = mine.astype(jnp.float32)
    normed_input = (
        (own_cols - row_mean[:, None]) * lax.rsqrt(row_var + epsilon)[:, None] * ln_gain
    ).astype(jnp.bfloat16)
    qkv_part = jnp.einsum("td,dke->tke", normed_input, w_qkv, preferred_element_type=jnp.float32)
    up_part = jnp.dot(normed_input, w_up, preferred_element_type=jnp.float32)
    qkv_share, up_share = (
        lax.psum_scatter(
            qkv_part.astype(jnp.bfloat16), "chan", scatter_dimension=0, tiled=True
        ).astype(jnp.float32),
        lax.psum_scatter(
            up_part.astype(jnp.bfloat16), "chan", scatter_dimension=0, tiled=True
        ).astype(jnp.float32),
    )
    query_share, key_share, value_share, hidden_share = finish_rows(
        qkv_share, up_share, b_up, heads_dev
    )
    query_rows, key_rows, value_rows, hidden = (
        lax.all_gather(query_share, "chan", axis=0, tiled=True),
        lax.all_gather(key_share, "chan", axis=0, tiled=True),
        lax.all_gather(value_share, "chan", axis=0, tiled=True),
        lax.all_gather(hidden_share, "chan", axis=0, tiled=True),
    )
    images = tok_count // PATCHES
    queries = query_rows.reshape(images, PATCHES, heads_dev, HS)
    keys = key_rows.reshape(images, PATCHES, heads_dev, HS)
    values = value_rows.reshape(images, PATCHES, heads_dev, HS)
    scores = jnp.einsum("bqhe,bkhe->bhqk", queries, keys, preferred_element_type=jnp.float32) * (
        2.0 / math.sqrt(HS)
    )
    expo = jnp.exp(scores)
    probs = (expo / jnp.sum(expo, axis=-1, keepdims=True)).astype(jnp.bfloat16)
    attended = jnp.einsum("bhqk,bkhe->bqhe", probs, values, preferred_element_type=jnp.float32)
    attended = attended.astype(jnp.bfloat16).reshape(tok_count, width_hid)
    term = jnp.dot(attended, w_out, preferred_element_type=jnp.float32) + jnp.dot(
        hidden, w_down, preferred_element_type=jnp.float32
    )
    mixed = lax.psum(term, "hid")
    return (own_cols + mixed).astype(jnp.bfloat16)


def solution(mesh):
    in_specs = (
        P("chan", None, None),
        P("chan", None, "hid"),
        P("chan", "hid"),
        P("chan", "hid"),
        P("chan", "hid"),
        P("chan"),
        P("chan"),
        P("chan", None, "hid"),
        P("chan", "hid"),
        P("hid"),
        P("hid", "chan"),
        P("hid", "chan"),
    )
    out_specs = P(None, "chan")
    return jax.shard_map(
        on_device, mesh=mesh, in_specs=in_specs, out_specs=out_specs, check_vma=False
    )
```

profile of v0, /device:TPU:0, one launch (start us, length us, event | category | flops | bytes accessed | tf_op | source)
XLA Modules:
  0.0 780.2 jit_solution(2045412981143405703)
XLA Ops:
  11.8 171.0 %fusion.1 = f32[96,256,768]{2,1,0:T(8,128)} fusion(f32[96,768]{1,0:T(8,128)S(1)} %convert_element_type.64, bf16[96,256,256]{2,1,0:T(8,128)(2,1)} %param.12, bf16[96,256,768]{2,1,0:T(8,128)(2,1)} %param.13), kind=kOutput, calls=%fused_computation.2 | convolution fusion | flops 10890510336 | bytes 126124032 | tf_op jit(solution)/shard_map/ctp,cpd->ctd/dot_general | solution.py:58
  182.8 72.9 %copy.57 = f32[96,256,768]{1,2,0:T(8,128)} copy(f32[96,256,768]{2,1,0:T(8,128)} %fusion.1) | data formatting | bytes 150994944 | tf_op jit(solution)/shard_map/mul | solution.py:60
  255.7 23.3 %multiply_reduce_fusion = f32[96,256,6]{1,2,0:T(8,128)S(1)} fusion(f32[96,256,6,128]{1,3,2,0:T(8,128)} %bitcast.4), kind=kLoop, calls=%fused_computation.5 | loop fusion | flops 37601280 | bytes 76087296 | tf_op jit(solution)/shard_map/reduce_sum | solution.py:17
  279.1 43.4 %fusion.2 = f32[96,6,1,256]{3,2,1,0:T(1,128)S(1)} fusion(f32[96,6,128,1]{2,3,1,0:T(1,128)S(1)} %copy-done.1, f32[96,256,6,128]{1,3,2,0:T(8,128)} %bitcast.4, f32[96,256,6]{1,2,0:T(8,128)S(1)} %add_rsqrt_fusion), kind=kOutput, calls=%fused_computation.3 | convolution fusion | flops 245366784 | bytes 76972032 | tf_op jit(solution)/shard_map/cthe,che->cth/dot_general | solution.py:69
  323.4 48.9 %broadcast_multiply_fusion = f32[96,256,6,128]{1,3,2,0:T(8,128)} fusion(f32[96,256,6,128]{1,3,2,0:T(8,128)} %bitcast.4, f32[96,256,6]{1,2,0:T(8,128)S(1)} %copy.59), kind=kLoop, calls=%fused_computation.21 | loop fusion | flops 18874368 | bytes 151584768 | tf_op jit(solution)/shard_map/mul | solution.py:75
  372.3 74.2 %copy.60 = f32[96,256,6,128]{3,0,2,1:T(8,128)} copy(f32[96,256,6,128]{1,3,2,0:T(8,128)} %broadcast_multiply_fusion) | data formatting | bytes 150994944 | tf_op jit(solution)/shard_map/mul | solution.py:75
  446.9 34.5 %broadcast_divide_fusion = f32[12,256,6,128]{3,0,2,1:T(8,128)} fusion(f32[12,256,6]{0,2,1:T(8,128)S(1)} %copy.61, f32[96,256,6,128]{3,0,2,1:T(8,128)} %copy.60, s32[96]{0:T(128)} %copy-done.5), kind=kOutput, calls=%fused_computation.28 | convolution fusion | flops 2720269312 | bytes 85008768 | tf_op jit(solution)/shard_map/kc,cthe->kthe/dot_general | solution.py:74
  481.4 12.1 %copy.86 = f32[12,256,6,128]{1,3,2,0:T(8,128)} copy(f32[12,256,6,128]{3,0,2,1:T(8,128)} %broadcast_divide_fusion) | data formatting | bytes 18874368
  493.5 5.0 fusion.12
  499.5 47.0 %all-reduce.3.cloned.1.call-done = bf16[256,768]{1,0:T(8,128)(2,1)} async-done(((bf16[256,768]{1,0:T(8,128)(2,1)}), bf16[256,768]{1,0:T(8,128)(2,1)}) %all-reduce.3.cloned.1.call-update) | async-done | bytes 393232 | tf_op jit(solution)/shard_map/psum | solution.py:82
  546.5 39.8 %all-gather.4.cloned.1.call-done = bf16[256,6144]{1,0:T(8,128)(2,1)} async-done(((bf16[256,768]{1,0:T(8,128)(2,1)}), bf16[256,6144]{1,0:T(8,128)(2,1)}) %all-gather.4.cloned.1.call-update) | async-done | bytes 3145744 | tf_op jit(solution)/shard_map/all_gather | solution.py:83
  586.3 3.2 convert_reduce_fusion
  589.5 7.8 %convolution_convert_fusion = bf16[256,3072]{1,0:T(8,128)(2,1)} fusion(bf16[1536,3072]{1,0:T(8,128)(2,1)} %param.20, f32[1536]{0:T(1024)S(1)} %copy-done.7, f32[256]{0:T(256)S(1)} %get-tuple-element.12, f32[256]{0:T(256)S(1)} %get-tuple-element.11, bf16[256,6144]{1,0:T(8,128)(2,1)} %all-gather.4.cloned.1.call-done, s32[]{:T(128)S(6)} %select_n.3), kind=kOutput, calls=%fused_computation.29 | convolution fusion | flops 2418671616 | bytes 11804676 | tf_op jit(solution)/shard_map/dot_general | solution.py:95
  597.4 6.5 convolution_convert_fusion.1
  604.2 23.3 %reduce-scatter.5.cloned.1.call-done = bf16[64,3072]{1,0:T(8,128)(2,1)} async-done(((bf16[256,3072]{1,0:T(8,128)(2,1)}), bf16[64,3072]{1,0:T(8,128)(2,1)}) %reduce-scatter.5.cloned.1.call-update) | async-done | bytes 393232 | tf_op jit(solution)/shard_map/reduce_scatter | solution.py:100
  627.6 3.5 fusion.20
  631.1 28.0 %reduce-scatter.3.cloned.1.call-done = bf16[64,3,768]{2,0,1:T(8,128)(2,1)} async-done(((bf16[256,3,768]{2,0,1:T(8,128)(2,1)}), bf16[64,3,768]{2,0,1:T(8,128)(2,1)}) %reduce-scatter.3.cloned.1.call-update) | async-done | bytes 294928 | tf_op jit(solution)/shard_map/reduce_scatter | solution.py:97
  660.0 9.5 %all-gather = bf16[256,1,768]{2,0,1:T(8,128)(2,1)S(1)} all-gather(bf16[64,1,768]{2,0,1:T(8,128)(2,1)S(1)} %slice.13), channel_id=2, replica_groups=mesh['chan'=4,'hid'=8] {'chan'}, dimensions={0}, use_global_device_ids=true | all-gather | bytes 491520 | tf_op jit(solution)/shard_map/all_gather | solution.py:110
  674.9 10.6 %all_gather.18 = bf16[256,768]{1,0:T(8,128)(2,1)S(1)} all-gather(bf16[64,768]{1,0:T(8,128)(2,1)S(1)} %get-tuple-element.7), channel_id=1, replica_groups=mesh['chan'=4,'hid'=8] {'chan'}, dimensions={0}, use_global_device_ids=true | all-gather | bytes 491520 | tf_op jit(solution)/shard_map/all_gather | solution.py:109
  685.6 11.0 %all_gather.17 = bf16[256,768]{1,0:T(8,128)(2,1)S(1)} all-gather(bf16[64,768]{1,0:T(8,128)(2,1)} %get-tuple-element.8), channel_id=1, replica_groups=mesh['chan'=4,'hid'=8] {'chan'}, dimensions={0}, use_global_device_ids=true | all-gather | bytes 491520 | tf_op jit(solution)/shard_map/all_gather | solution.py:108
  698.4 2.4 convolution_convert_fusion.2
  700.8 5.7 fusion.50
  708.5 62.2 %all-reduce.5.cloned.1.call-done = f32[256,1536]{1,0:T(8,128)} async-done(((f32[256,1536]{1,0:T(8,128)}), f32[256,1536]{1,0:T(8,128)}) %all-reduce.5.cloned.1.call-update) | async-done | bytes 1572880 | tf_op jit(solution)/shard_map/psum | solution.py:127
  770.6 2.7 fusion.17
  (66 shorter events, 18.2 us)
Async XLA Ops:
  6.5 699.9 %copy-start = (bf16[768,1536]{1,0:T(8,128)(2,1)S(1)}, bf16[768,1536]{1,0:T(8,128)(2,1)}, u32[]{:S(2)}) copy-start(bf16[768,1536]{1,0:T(8,128)(2,1)} %param.22) | copy-start | bytes 7077892
  6.5 539.9 %all-reduce.3.cloned.1.call-start = ((), (), s32[]{:S(2)}) async-start(), calls=%async_computation.2 | async-start | bytes 786432 | tf_op jit(solution)/shard_map/psum | solution.py:82
  7.3 0.6 copy-start.5
  255.7 23.4 %copy-start.1 = (f32[96,6,128,1]{2,3,1,0:T(1,128)S(1)}, f32[96,6,128,1]{2,3,1,0:T(1,128)}, u32[]{:S(2)}) copy-start(f32[96,6,128,1]{2,3,1,0:T(1,128)} %reshape.112) | copy-start | bytes 884740
  255.7 66.8 %copy-start.3 = (f32[96,6]{0,1:T(8,128)S(1)}, f32[96,6]{0,1:T(8,128)}, u32[]{:S(2)}) copy-start(f32[96,6]{0,1:T(8,128)} %sqrt.7) | copy-start | bytes 6916
  255.7 67.0 %copy-start.6 = (s32[96]{0:T(128)S(1)}, s32[96]{0:T(128)}, u32[]{:S(2)}) copy-start(s32[96]{0:T(128)} %copy-done.5) | copy-start | bytes 1156
  279.0 44.4 %copy-start.2 = (bf16[12,768]{1,0:T(8,128)(2,1)S(1)}, bf16[12,768]{1,0:T(8,128)(2,1)}, u32[]{:S(2)}) copy-start(bf16[12,768]{1,0:T(8,128)(2,1)} %param.16) | copy-start | bytes 55300
  446.9 142.7 %copy-start.7 = (f32[1536]{0:T(1024)S(1)}, f32[1536]{0:T(1024)}, u32[]{:S(2)}) copy-start(f32[1536]{0:T(1024)} %param.18) | copy-start | bytes 18436
  446.9 180.7 %copy-start.4 = (f32[3072]{0:T(1024)S(1)}, f32[3072]{0:T(1024)}, u32[]{:S(2)}) copy-start(f32[3072]{0:T(1024)} %param.21) | copy-start | bytes 36868
  499.5 86.9 %all-gather.4.cloned.1.call-start = ((), (), s32[]{:S(2)}) async-start(), calls=%async_computation.3 | async-start | bytes 3538944 | tf_op jit(solution)/shard_map/all_gather | solution.py:83
  546.5 81.1 %reduce-scatter.5.cloned.1.call-start = ((), (), s32[]{:S(2)}) async-start(), calls=%async_computation.5 | async-start | bytes 1966080 | tf_op jit(solution)/shard_map/reduce_scatter | solution.py:100
  597.4 61.7 %reduce-scatter.3.cloned.1.call-start = ((), (), s32[]{:S(2)}) async-start(), calls=%async_computation.4 | async-start | bytes 1474560 | tf_op jit(solution)/shard_map/reduce_scatter | solution.py:97
  603.9 96.9 %all-gather.6.cloned.1.call-start = ((), (), s32[]{:S(2)}) async-start(), calls=%async_computation.6 | async-start | bytes 1966080 | tf_op jit(solution)/shard_map/all_gather | solution.py:111
  631.1 139.6 %all-reduce.5.cloned.1.call-start = ((), (), s32[]{:S(2)}) async-start(), calls=%async_computation.7 | async-start | bytes 3145728 | tf_op jit(solution)/shard_map/psum | solution.py:127
Sparse Core Ops, SparseCore 0:
  499.6 46.8 all-reduce.2
  548.1 38.1 all-gather.3
  597.5 30.0 reduce-scatter.4
  630.3 28.7 reduce-scatter.2
  660.8 33.7 all-gather.5
  708.6 61.9 all-reduce.4
where the time goes:
time: 783 us; the launch traced here: 780 us
  matrix products  276 us (35%)
  waiting for transfers between devices  200 us (26%)
  local copies, waits for them, and re-layouts  167 us (21%)
  other arithmetic  91.4 us (12%)
  blocking collectives  31.1 us (4%)
  between operations  13.7 us (2%)
    dot_general x1, matrix products, on_device(): jnp.einsum('ctp,cpd->ctd', pixels, patch_weight, preferred_element_type=j...  171 us
    mul x1, local copies, waits for them, and re-layouts, on_device(): weight[..., None] * split  74.2 us
    mul x1, local copies, waits for them, and re-layouts, on_device(): features = jax.nn.gelu(embedded, approximate=False)  72.9 us
    psum x1, waiting for transfers between devices, on_device(): mixed = lax.psum(term, 'hid')  62.2 us
    mul x1, other arithmetic, on_device(): weight[..., None] * split  48.9 us
    psum x1, waiting for transfers between devices, on_device(): layer_sum = lax.psum(partial_value.astype(jnp.bfloat16), 'chan')  47 us
    dot_general x1, matrix products, on_device(): jnp.einsum('cthe,che->cth', normed, query, precision=lax.Precision.HIGHEST)  43.4 us
    all_gather x1, waiting for transfers between devices, on_device(): gathered = lax.all_gather(layer_sum, 'hid', axis=1, tiled=True)  39.8 us
  transfers between devices with their start and end apart: 6, of which 5 were waited for; matrix products, arithmetic and copies ran while one was open for 3% of the time, Pallas kernels for 0%

commit v1 on v0

--- a/solution.py
+++ b/solution.py
@@ -1,8 +1,11 @@
+import functools
 import math
 
 import jax
 import jax.numpy as jnp
 from jax import lax
+from jax.experimental import pallas as pl
+from jax.experimental.pallas import tpu as pltpu
 from jax.sharding import PartitionSpec as P
 
 HS = 128
@@ -11,6 +14,94 @@
 
 
 epsilon = 1e-06
+
+
+def pool_kernel(size, order_ref, pix_ref, pw_ref, emb_ref, qb_ref, shift_ref, mix_ref, out_ref, feat, sq, numer, denom, acc):
+    g = pl.program_id(0); j = pl.program_id(1)
+    tok, width = acc.shape
+    heads = width // HS
+    lane = feat.shape[1]
+    rows = lax.broadcasted_iota(jnp.int32, (width, HS), 0) // HS
+    cols = lax.broadcasted_iota(jnp.int32, (width, HS), 1)
+    pick = (rows == cols).astype(jnp.bfloat16)
+
+    @pl.when((g == 0) & (j == 0))
+    def _():
+        acc[...] = jnp.zeros_like(acc)
+
+    step = min(256, width)
+    for n in range(width // step):
+        cs = slice(n * step, (n + 1) * step)
+        for r in range(0, tok, 64):
+            e = jnp.dot(pix_ref[0, r:r+64], pw_ref[0, :, cs], preferred_element_type=jnp.float32)
+            e = e + emb_ref[0, :, cs]
+            f = (0.5 * e) * (1.0 + lax.erf(e * math.sqrt(0.5)))
+            feat[r:r+64, cs] = f.astype(jnp.bfloat16)
+            sq[r:r+64, cs] = (f * f).astype(jnp.bfloat16)
+    dots = jnp.dot(feat[...], qb_ref[0], preferred_element_type=jnp.float32)
+    total = jnp.dot(sq[...], pick, preferred_element_type=jnp.float32)
+    score = dots * lax.rsqrt(total * (1.0 / HS) + epsilon) * (1.0 / math.sqrt(HS))
+    weight = jnp.exp(score - shift_ref[0])
+    @pl.when(j == 0)
+    def _():
+        denom[...] = weight
+        for h in range(heads):
+            hs = slice(h * HS, (h + 1) * HS)
+            numer[:, hs] = weight[:, h:h+1] * feat[:, hs].astype(jnp.float32)
+    @pl.when(j > 0)
+    def _():
+        denom[...] += weight
+        for h in range(heads):
+            hs = slice(h * HS, (h + 1) * HS)
+            numer[:, hs] += weight[:, h:h+1] * feat[:, hs].astype(jnp.float32)
+    @pl.when(j == size - 1)
+    def _():
+        inv = 1.0 / denom[...]
+        for h in range(heads):
+            hs = slice(h * HS, (h + 1) * HS)
+            acc[:, hs] += numer[:, hs] * inv[:, h:h+1] * mix_ref[0, :, hs]
+    @pl.when((g == pl.num_programs(0) - 1) & (j == size - 1))
+    def _():
+        out_ref[...] = acc[...].astype(jnp.bfloat16)
+
+def pool(pixels, patch_weight, channel_embed, pool_query, group_mix, assign):
+    chans, tok, p2 = pixels.shape
+    width = patch_weight.shape[2]
+    groups = pool_query.shape[0]
+    size = chans // groups
+    heads = width // HS
+    idx = jnp.arange(chans, dtype=jnp.int32)
+    key = assign * chans + idx
+    rank = jnp.sum((key[None, :] < key[:, None]).astype(jnp.int32), axis=1)
+    order = jnp.sum(jnp.where(rank[None, :] == idx[:, None], idx[None, :], 0), axis=1).astype(jnp.int32)
+    q = pool_query.astype(jnp.float32)
+    heads_of = jnp.arange(width, dtype=jnp.int32) // HS
+    lanes = jnp.arange(HS, dtype=jnp.int32)
+    qb = jnp.where(heads_of[None, :, None] == lanes[None, None, :], pool_query[:, :, None], jnp.bfloat16(0))
+    sh = jnp.sqrt(jnp.sum((q * q).reshape(groups, heads, HS), axis=-1))
+    sh = jnp.pad(sh, ((0, 0), (0, HS - heads))).reshape(groups, 1, HS)
+    spec = pltpu.PrefetchScalarGridSpec(
+        num_scalar_prefetch=1, grid=(groups, size),
+        in_specs=[
+            pl.BlockSpec((1, tok, p2), lambda g, j, o: (o[g * size + j], 0, 0)),
+            pl.BlockSpec((1, p2, width), lambda g, j, o: (o[g * size + j], 0, 0)),
+            pl.BlockSpec((1, 1, width), lambda g, j, o: (o[g * size + j], 0, 0)),
+            pl.BlockSpec((1, width, HS), lambda g, j, o: (g, 0, 0)),
+            pl.BlockSpec((1, 1, HS), lambda g, j, o: (g, 0, 0)),
+            pl.BlockSpec((1, 1, width), lambda g, j, o: (g, 0, 0)),
+        ],
+        out_specs=pl.BlockSpec((tok, width), lambda g, j, o: (0, 0)),
+        scratch_shapes=[
+            pltpu.VMEM((tok, width), jnp.bfloat16), pltpu.VMEM((tok, width), jnp.bfloat16),
+            pltpu.VMEM((tok, width), jnp.float32), pltpu.VMEM((tok, HS), jnp.float32),
+            pltpu.VMEM((tok, width), jnp.float32)])
+    return pl.pallas_call(
+        functools.partial(pool_kernel, size), grid_spec=spec,
+        out_shape=jax.ShapeDtypeStruct((tok, width), jnp.bfloat16),
+        compiler_params=pltpu.CompilerParams(dimension_semantics=("arbitrary", "arbitrary"), vmem_limit_bytes=40 << 20),
+        name="pool",
+    )(order, pixels, patch_weight, channel_embed.astype(jnp.float32).reshape(chans, 1, width), qb, sh,
+      group_mix.astype(jnp.float32).reshape(groups, 1, width))
 
 
 def head_norm(values):
@@ -49,36 +140,11 @@
     w_out,
     w_down,
 ):
-    chan_count = pixels.shape[0]
     tok_count = pixels.shape[1]
     width_hid = patch_weight.shape[2]
     width_chan = ln_gain.shape[0]
     heads_dev = width_hid // HS
-    groups_dev = pool_query.shape[0]
-    embedded = jnp.einsum("ctp,cpd->ctd", pixels, patch_weight, preferred_element_type=jnp.float32)
-    embedded = embedded + channel_embed.astype(jnp.float32)[:, None, :]
-    features = jax.nn.gelu(embedded, approximate=False)
-    split = features.reshape(chan_count, tok_count, heads_dev, HS)
-    normed = head_norm(split)
-    local_group = assign - lax.axis_index("chan") * groups_dev
-    member = (local_group[None, :] == jnp.arange(groups_dev, dtype=jnp.int32)[:, None]).astype(
-        jnp.float32
-    )
-    query = jnp.dot(member.T, pool_query.astype(jnp.float32), precision=lax.Precision.HIGHEST)
-    query = query.reshape(chan_count, heads_dev, HS)
-    score = jnp.einsum("cthe,che->cth", normed, query, precision=lax.Precision.HIGHEST) / math.sqrt(
-        HS
-    )
-    shift = jnp.sqrt(jnp.sum(query * query, axis=-1))
-    weight = jnp.exp(score - shift[:, None, :])
-    numer = jnp.einsum(
-        "kc,cthe->kthe", member, weight[..., None] * split, precision=lax.Precision.HIGHEST
-    )
-    denom = jnp.einsum("kc,cth->kth", member, weight, precision=lax.Precision.HIGHEST)
-    pooled = (numer / denom[..., None]).reshape(groups_dev, tok_count, width_hid)
-    partial_value = jnp.einsum(
-        "kd,ktd->td", group_mix.astype(jnp.float32), pooled, precision=lax.Precision.HIGHEST
-    )
+    partial_value = pool(pixels, patch_weight, channel_embed, pool_query, group_mix, assign)
     layer_sum = lax.psum(partial_value.astype(jnp.bfloat16), "chan")
     gathered = lax.all_gather(layer_sum, "hid", axis=1, tiled=True)
     wide = gathered.astype(jnp.float32)
@@ -124,7 +190,7 @@
     term = jnp.dot(attended, w_out, preferred_element_type=jnp.float32) + jnp.dot(
         hidden, w_down, preferred_element_type=jnp.float32
     )
-    mixed = lax.psum(term, "hid")
+    mixed = lax.psum(term.astype(jnp.bfloat16), "hid").astype(jnp.float32)
     return (own_cols + mixed).astype(jnp.bfloat16)
 
 

time: 783 us -> 396 us (0.51)
  matrix products: 276 us -> 25.6 us
  local copies, waits for them, and re-layouts: 167 us -> 5.74 us
  Pallas kernels: 0 us -> 106 us
  other arithmetic: 91.4 us -> 15.4 us
    dot_general x5 -> x0, matrix products: 250 us -> none  [the longest x1 171 us: on_device(): jnp.einsum('ctp,cpd->ctd', pixels, patch_weight, preferred_element_type=j...]
    mul x2 -> x0, local copies, waits for them, and re-layouts: 147 us -> none  [the longest x1 74.2 us: on_device(): weight[..., None] * split]
    pallas_call x0 -> x1, Pallas kernels: none -> 106 us  [pool(): pl.pallas_call(functools.partial(pool_kernel, size), grid_spec=spec, out_...]
    mul x1, other arithmetic: 48.9 us -> 0.75 us  [pool(): sh = jnp.sqrt(jnp.sum((q * q).reshape(groups, heads, HS), axis=-1))]
    reduce_sum x3 -> x2, other arithmetic: 23.6 us -> 0.28 us  [head_norm(): jnp.mean(values * values, axis=-1, keepdims=True) + epsilon]
    unnamed x17 -> x10, local copies, waits for them, and re-layouts: 12.8 us -> 0.02 us
  transfers between devices with their start and end apart: 6 -> 6, of which waited for: 5 -> 5; matrix products, arithmetic and copies ran while one was open for 3% -> 5% of each run, Pallas kernels for 0% -> 0%
where the time goes in v1:
time: 396 us; the launch traced here: 393 us
  waiting for transfers between devices  196 us (49%)
  Pallas kernels  106 us (27%)
  blocking collectives  31.2 us (8%)
  matrix products  25.6 us (6%)
  other arithmetic  15.4 us (4%)
  between operations  13.7 us (3%)
  local copies, waits for them, and re-layouts  5.74 us (1%)
    pallas_call x1, Pallas kernels, pool(): pl.pallas_call(functools.partial(pool_kernel, size), grid_spec=spec, out_...  106 us
    psum x1, waiting for transfers between devices, on_device(): mixed = lax.psum(term.astype(jnp.bfloat16), 'hid').astype(jnp.float32)  57.2 us
    psum x1, waiting for transfers between devices, on_device(): layer_sum = lax.psum(partial_value.astype(jnp.bfloat16), 'chan')  47 us
    all_gather x1, waiting for transfers between devices, on_device(): gathered = lax.all_gather(layer_sum, 'hid', axis=1, tiled=True)  39.8 us
    reduce_scatter x1, waiting for transfers between devices, on_device(): lax.psum_scatter(qkv_part.astype(jnp.bfloat16), 'chan', scatter_dimension...  28 us
    reduce_scatter x1, waiting for transfers between devices, on_device(): lax.psum_scatter(up_part.astype(jnp.bfloat16), 'chan', scatter_dimension=...  23.6 us
    all_gather x1, blocking collectives, on_device(): lax.all_gather(query_share, 'chan', axis=0, tiled=True)  11.9 us
    all_gather x1, blocking collectives, on_device(): lax.all_gather(key_share, 'chan', axis=0, tiled=True)  9.69 us
  transfers between devices with their start and end apart: 6, of which 5 were waited for; matrix products, arithmetic and copies ran while one was open for 5% of the time, Pallas kernels for 0%

profile of v1, /device:TPU:0, one launch (start us, length us, event | category | flops | bytes accessed | tf_op | source)
XLA Modules:
  0.0 393.3 jit_solution(14164936919204681920)
XLA Ops:
  6.5 0.8 iota_add_fusion
  9.5 1.1 reshape.138.emb_ref
  10.6 2.4 broadcast_select_fusion.qb_ref
  12.9 106.0 %pool.1 = bf16[256,768]{1,0:T(8,128)(2,1)} custom-call(s32[96]{0:T(128)S(1)} %select_reduce_fusion.order_ref, bf16[96,256,256]{2,1,0:T(8,128)(2,1)} %pix_ref.1, bf16[96,256,768]{2,1,0:T(8,128)(2,1)} %pw_ref.1, f32[96,1,768]{2,1,0:T(1,128)S(1)} %reshape.138.emb_ref, bf16[12,768,128]{2,1,0:T(8,128)(2,1)S(1)} %broadcast_select_fusion.qb_ref, ...), custom_call_target="tpu_custom_call" | custom-call | tf_op jit(solution)/shard_map/pool/pallas_call | solution.py:98
  119.0 47.0 %all-reduce.4.cloned.1.call-done = bf16[256,768]{1,0:T(8,128)(2,1)} async-done(((bf16[256,768]{1,0:T(8,128)(2,1)}), bf16[256,768]{1,0:T(8,128)(2,1)}) %all-reduce.4.cloned.1.call-update) | async-done | bytes 393232 | tf_op jit(solution)/shard_map/psum | solution.py:148
  166.0 39.8 %all-gather.4.cloned.1.call-done = bf16[256,6144]{1,0:T(8,128)(2,1)} async-done(((bf16[256,768]{1,0:T(8,128)(2,1)}), bf16[256,6144]{1,0:T(8,128)(2,1)}) %all-gather.4.cloned.1.call-update) | async-done | bytes 3145744 | tf_op jit(solution)/shard_map/all_gather | solution.py:149
  205.8 3.2 convert_reduce_fusion
  209.0 7.8 %convolution_convert_fusion = bf16[256,3072]{1,0:T(8,128)(2,1)} fusion(bf16[1536,3072]{1,0:T(8,128)(2,1)} %param.20, f32[1536]{0:T(1024)S(1)} %copy-done.4, f32[256]{0:T(256)S(1)} %get-tuple-element.12, f32[256]{0:T(256)S(1)} %get-tuple-element.11, bf16[256,6144]{1,0:T(8,128)(2,1)} %all-gather.4.cloned.1.call-done, s32[]{:T(128)S(6)} %select_n.23), kind=kOutput, calls=%fused_computation.3 | convolution fusion | flops 2418671616 | bytes 11804676 | tf_op jit(solution)/shard_map/dot_general | solution.py:161
  216.9 6.5 %convolution_convert_fusion.1 = bf16[256,3,768]{2,0,1:T(8,128)(2,1)} fusion(bf16[1536,3,768]{2,0,1:T(8,128)(2,1)} %param.19, f32[1536]{0:T(1024)S(1)} %copy-done.4, f32[256]{0:T(256)S(1)} %get-tuple-element.12, f32[256]{0:T(256)S(1)} %get-tuple-element.11, bf16[256,6144]{1,0:T(8,128)(2,1)} %all-gather.4.cloned.1.call-done, s32[]{:T(128)S(6)} %select_n.23), kind=kOutput, calls=%fused_computation.15 | convolution fusion | flops 1814495232 | bytes 9052164 | tf_op jit(solution)/shard_map/td,dke->tke/dot_general | solution.py:160
  223.5 23.6 %reduce-scatter.5.cloned.1.call-done = bf16[64,3072]{1,0:T(8,128)(2,1)} async-done(((bf16[256,3072]{1,0:T(8,128)(2,1)}), bf16[64,3072]{1,0:T(8,128)(2,1)}) %reduce-scatter.5.cloned.1.call-update) | async-done | bytes 393232 | tf_op jit(solution)/shard_map/reduce_scatter | solution.py:166
  247.1 3.5 fusion.8
  250.6 28.0 %reduce-scatter.3.cloned.1.call-done = bf16[64,3,768]{2,0,1:T(8,128)(2,1)} async-done(((bf16[256,3,768]{2,0,1:T(8,128)(2,1)}), bf16[64,3,768]{2,0,1:T(8,128)(2,1)}) %reduce-scatter.3.cloned.1.call-update) | async-done | bytes 294928 | tf_op jit(solution)/shard_map/reduce_scatter | solution.py:163
  278.6 1.0 slice.13
  279.6 9.5 %all-gather = bf16[256,1,768]{2,0,1:T(8,128)(2,1)S(1)} all-gather(bf16[64,1,768]{2,0,1:T(8,128)(2,1)S(1)} %slice.13), channel_id=2, replica_groups=mesh['chan'=4,'hid'=8] {'chan'}, dimensions={0}, use_global_device_ids=true | all-gather | bytes 491520 | tf_op jit(solution)/shard_map/all_gather | solution.py:176
  289.1 0.9 copy.37
  290.8 1.0 mul.118
  293.5 9.7 %all_gather.18 = bf16[256,768]{1,0:T(8,128)(2,1)S(1)} all-gather(bf16[64,768]{1,0:T(8,128)(2,1)S(1)} %get-tuple-element.7), channel_id=1, replica_groups=mesh['chan'=4,'hid'=8] {'chan'}, dimensions={0}, use_global_device_ids=true | all-gather | bytes 491520 | tf_op jit(solution)/shard_map/all_gather | solution.py:175
  303.3 11.9 %all_gather.17 = bf16[256,768]{1,0:T(8,128)(2,1)S(1)} all-gather(bf16[64,768]{1,0:T(8,128)(2,1)} %get-tuple-element.8), channel_id=1, replica_groups=mesh['chan'=4,'hid'=8] {'chan'}, dimensions={0}, use_global_device_ids=true | all-gather | bytes 491520 | tf_op jit(solution)/shard_map/all_gather | solution.py:174
  315.5 1.6 multiply_exponential_fusion
  317.1 2.4 convolution_convert_fusion.2
  319.5 5.7 %fusion.29 = f32[256,1536]{1,0:T(8,128)S(1)} fusion(bf16[256,3072]{1,0:T(8,128)(2,1)} %all-gather.6.cloned.1.call-done, bf16[3072,1536]{1,0:T(8,128)(2,1)} %param.23), kind=kOutput, calls=%fused_computation.65 | convolution fusion | flops 2415919104 | bytes 12582912 | tf_op jit(solution)/shard_map/dot_general | solution.py:190
  325.1 1.7 fusion.1
  326.8 57.2 %all-reduce.6.cloned.1.call-done = bf16[256,1536]{1,0:T(8,128)(2,1)} async-done(((bf16[256,1536]{1,0:T(8,128)(2,1)}), bf16[256,1536]{1,0:T(8,128)(2,1)}) %all-reduce.6.cloned.1.call-update) | async-done | bytes 786448 | tf_op jit(solution)/shard_map/psum | solution.py:193
  384.0 2.4 fusion.5
  (51 shorter events, 5.2 us)
Async XLA Ops:
  6.5 318.6 %copy-start = (bf16[768,1536]{1,0:T(8,128)(2,1)S(1)}, bf16[768,1536]{1,0:T(8,128)(2,1)}, u32[]{:S(2)}) copy-start(bf16[768,1536]{1,0:T(8,128)(2,1)} %param.22) | copy-start | bytes 7077892
  6.5 159.4 %all-reduce.4.cloned.1.call-start = ((), (), s32[]{:S(2)}) async-start(), calls=%async_computation.2 | async-start | bytes 786432 | tf_op jit(solution)/shard_map/psum | solution.py:148
  118.9 86.9 %all-gather.4.cloned.1.call-start = ((), (), s32[]{:S(2)}) async-start(), calls=%async_computation.3 | async-start | bytes 3538944 | tf_op jit(solution)/shard_map/all_gather | solution.py:149
  166.0 81.1 %reduce-scatter.5.cloned.1.call-start = ((), (), s32[]{:S(2)}) async-start(), calls=%async_computation.5 | async-start | bytes 1966080 | tf_op jit(solution)/shard_map/reduce_scatter | solution.py:166
  166.0 43.0 %copy-start.4 = (f32[1536]{0:T(1024)S(1)}, f32[1536]{0:T(1024)}, u32[]{:S(2)}) copy-start(f32[1536]{0:T(1024)} %param.18) | copy-start | bytes 18436
  216.9 30.2 %copy-start.3 = (f32[3072]{0:T(1024)S(1)}, f32[3072]{0:T(1024)}, u32[]{:S(2)}) copy-start(f32[3072]{0:T(1024)} %param.21) | copy-start | bytes 36868
  216.9 61.7 %reduce-scatter.3.cloned.1.call-start = ((), (), s32[]{:S(2)}) async-start(), calls=%async_computation.4 | async-start | bytes 1474560 | tf_op jit(solution)/shard_map/reduce_scatter | solution.py:163
  223.4 96.0 %all-gather.6.cloned.1.call-start = ((), (), s32[]{:S(2)}) async-start(), calls=%async_computation.6 | async-start | bytes 1966080 | tf_op jit(solution)/shard_map/all_gather | solution.py:177
  250.5 133.5 %all-reduce.6.cloned.1.call-start = ((), (), s32[]{:S(2)}) async-start(), calls=%async_computation.7 | async-start | bytes 1572864 | tf_op jit(solution)/shard_map/psum | solution.py:193
  278.6 11.5 %copy-start.1 = (bf16[64,3,768]{2,0,1:T(8,128)(2,1)S(1)}, bf16[64,3,768]{2,0,1:T(8,128)(2,1)}, u32[]{:S(2)}) copy-start(bf16[64,3,768]{2,0,1:T(8,128)(2,1)} %reduce-scatter.3.cloned.1.call-done) | copy-start | bytes 884740
  315.5 1.6 copy-start.2
Sparse Core Ops, SparseCore 0:
  119.1 46.8 all-reduce.3
  167.6 38.1 all-gather.3
  217.0 30.0 reduce-scatter.4
  249.8 28.7 reduce-scatter.2
  280.3 33.4 all-gather.5
  327.0 57.0 all-reduce.5

commit v2 on v1

v2 whole, which is shorter than its diff:
```python
import functools
import math

import jax
import jax.numpy as jnp
from jax import lax
from jax.experimental import pallas as pl
from jax.experimental.pallas import tpu as pltpu
from jax.sharding import PartitionSpec as P

HS = 128
PATCHES = 256


epsilon = 1e-06


def pool_kernel(size, order_ref, pix_ref, pw_ref, emb_ref, query_ref, shift_ref, mix_ref, out_ref, feat, sq, numer, denom, acc, pick, quer):
    g = pl.program_id(0); j = pl.program_id(1)
    tok, width = acc.shape
    heads = width // HS
    head = lax.broadcasted_iota(jnp.int32, (HS, width), 0)
    head_of = lax.broadcasted_iota(jnp.int32, (HS, width), 1) // HS

    @pl.when((g == 0) & (j == 0))
    def _():
        acc[...] = jnp.zeros_like(acc)
        pick[...] = jnp.where(head_of == head, 1.0, 0.0).astype(jnp.bfloat16)

    @pl.when(j == 0)
    def _():
        quer[...] = jnp.where(head_of == head, query_ref[0], 0.0).astype(jnp.bfloat16)

    across = (((1,), (1,)), ((), ()))
    step = min(256, width)
    for n in range(width // step):
        cs = slice(n * step, (n + 1) * step)
        for r in range(0, tok, 64):
            e = jnp.dot(pix_ref[0, r:r+64], pw_ref[0, :, cs], preferred_element_type=jnp.float32)
            e = e + emb_ref[0, :, cs]
            f = (0.5 * e) * (1.0 + lax.erf(e * math.sqrt(0.5)))
            feat[r:r+64, cs] = f.astype(jnp.bfloat16)
            sq[r:r+64, cs] = (f * f).astype(jnp.bfloat16)
    dots = lax.dot_general(feat[...], quer[...], across, preferred_element_type=jnp.float32)
    total = lax.dot_general(sq[...], pick[...], across, preferred_element_type=jnp.float32)
    score = dots * lax.rsqrt(total * (1.0 / HS) + epsilon) * (1.0 / math.sqrt(HS))
    weight = jnp.exp(score - shift_ref[0])
    @pl.when(j == 0)
    def _():
        denom[...] = weight
        for h in range(heads):
            hs = slice(h * HS, (h + 1) * HS)
            numer[:, hs] = weight[:, h:h+1] * feat[:, hs].astype(jnp.float32)
    @pl.when(j > 0)
    def _():
        denom[...] += weight
        for h in range(heads):
            hs = slice(h * HS, (h + 1) * HS)
            numer[:, hs] += weight[:, h:h+1] * feat[:, hs].astype(jnp.float32)
    @pl.when(j == size - 1)
    def _():
        inv = 1.0 / denom[...]
        for h in range(heads):
            hs = slice(h * HS, (h + 1) * HS)
            acc[:, hs] += numer[:, hs] * inv[:, h:h+1] * mix_ref[0, :, hs]
    @pl.when((g == pl.num_programs(0) - 1) & (j == size - 1))
    def _():
        out_ref[...] = acc[...].astype(jnp.bfloat16)

def pool(pixels, patch_weight, channel_embed, pool_query, group_mix, assign):
    chans, tok, p2 = pixels.shape
    width = patch_weight.shape[2]
    groups = pool_query.shape[0]
    size = chans // groups
    heads = width // HS
    idx = jnp.arange(chans, dtype=jnp.int32)
    key = assign * chans + idx
    rank = jnp.sum((key[None, :] < key[:, None]).astype(jnp.int32), axis=1)
    order = jnp.sum(jnp.where(rank[None, :] == idx[:, None], idx[None, :], 0), axis=1).astype(jnp.int32)
    q = pool_query.astype(jnp.float32)
    sh = jnp.sqrt(jnp.sum((q * q).reshape(groups, heads, HS), axis=-1))
    sh = jnp.pad(sh, ((0, 0), (0, HS - heads))).reshape(groups, 1, HS)
    spec = pltpu.PrefetchScalarGridSpec(
        num_scalar_prefetch=1, grid=(groups, size),
        in_specs=[
            pl.BlockSpec((1, tok, p2), lambda g, j, o: (o[g * size + j], 0, 0)),
            pl.BlockSpec((1, p2, width), lambda g, j, o: (o[g * size + j], 0, 0)),
            pl.BlockSpec((1, 1, width), lambda g, j, o: (o[g * size + j], 0, 0)),
            pl.BlockSpec((1, 1, width), lambda g, j, o: (g, 0, 0)),
            pl.BlockSpec((1, 1, HS), lambda g, j, o: (g, 0, 0)),
            pl.BlockSpec((1, 1, width), lambda g, j, o: (g, 0, 0)),
        ],
        out_specs=pl.BlockSpec((tok, width), lambda g, j, o: (0, 0)),
        scratch_shapes=[
            pltpu.VMEM((tok, width), jnp.bfloat16), pltpu.VMEM((tok, width), jnp.bfloat16),
            pltpu.VMEM((tok, width), jnp.float32), pltpu.VMEM((tok, HS), jnp.float32),
            pltpu.VMEM((tok, width), jnp.float32), pltpu.VMEM((HS, width), jnp.bfloat16), pltpu.VMEM((HS, width), jnp.bfloat16)])
    return pl.pallas_call(
        functools.partial(pool_kernel, size), grid_spec=spec,
        out_shape=jax.ShapeDtypeStruct((tok, width), jnp.bfloat16),
        compiler_params=pltpu.CompilerParams(dimension_semantics=("arbitrary", "arbitrary"), vmem_limit_bytes=40 << 20),
        name="pool",
    )(order, pixels, patch_weight, channel_embed.astype(jnp.float32).reshape(chans, 1, width), q.reshape(groups, 1, width), sh,
      group_mix.astype(jnp.float32).reshape(groups, 1, width))


def head_norm(values):
    return values * lax.rsqrt(jnp.mean(values * values, axis=-1, keepdims=True) + epsilon)


MESH = pl.DeviceIdType.MESH


def greet(peers):
    gate = pltpu.get_barrier_semaphore()
    for peer in peers:
        pl.semaphore_signal(gate, inc=1, device_id=peer, device_id_type=MESH)
    pl.semaphore_wait(gate, len(peers))


def send(src, dst, sems, slot, peer):
    copy = pltpu.make_async_remote_copy(
        src_ref=src, dst_ref=dst, send_sem=sems.at[0, slot], recv_sem=sems.at[1, slot],
        device_id=peer, device_id_type=MESH)
    copy.start()
    return copy


def places(chans, hids):
    a, b = lax.axis_index("chan"), lax.axis_index("hid")
    chips, chip, core = hids // 2, b // 2, b % 2
    rows = [{"chan": lax.rem(a + k, chans)} for k in range(1, chans)]
    far = [{"hid": lax.rem(chip + k, chips) * 2 + core} for k in range(1, chips)]
    return a, b, chips, chip, core, rows, far, {"hid": chip * 2 + (1 - core)}


def spread(src_of, slots, chips, chip, core, far, mate, away, near):
    sent = [send(src_of(chip * 2 + core), src_of(chip * 2 + core), away, k, peer) for k, peer in enumerate(far)]
    mine = src_of(chip * 2 + core)
    passed = [send(mine, mine, near, 0, mate)]
    for k in range(1, chips):
        sent[k - 1].wait_recv()
        piece = src_of(lax.rem(chip + chips - k, chips) * 2 + core)
        passed.append(send(piece, piece, near, k, mate))
    for copy in passed:
        copy.wait()
    for copy in sent:
        copy.wait_send()


def layer_kernel(chans, hids, part, gain, normed_ref, own_ref, parts, gath, stat, whole, stats, s1, s2, s3, s4, s5):
    a, b, chips, chip, core, rows, far, mate = places(chans, hids)
    greet(rows + far + [mate])
    width = part.shape[2]
    size = part.shape[1]
    copies = [send(part.at[lax.rem(a + k, chans)], parts.at[k - 1], s1, k - 1, rows[k - 1]) for k in range(1, chans)]
    total = part[a].astype(jnp.float32)
    for k in range(chans - 1):
        copies[k].wait_recv()
        total = total + parts[k].astype(jnp.float32)
    gath[b] = total.astype(jnp.bfloat16)
    spread(lambda i: gath.at[i], None, chips, chip, core, far, mate, s2, s3)
    first = jnp.zeros((size, 1), jnp.float32)
    second = jnp.zeros((size, 1), jnp.float32)
    for i in range(hids):
        x = gath[i].astype(jnp.float32)
        first = first + jnp.sum(x, axis=1, keepdims=True)
        second = second + jnp.sum(x * x, axis=1, keepdims=True)
    mean = first / (width * hids)
    scale = lax.rsqrt(second / (width * hids) - mean * mean + epsilon)
    stat[...] = jnp.where(lax.broadcasted_iota(jnp.int32, stat.shape, 1) == 0, mean, scale)
    ratio = hids // chans
    moved = []
    for k in range(1, chans):
        to = lax.rem(a + k, chans)
        moved.append(send(stat, stats.at[a], s5, k - 1, rows[k - 1]))
        moved.append(send(gath.at[pl.ds(to * ratio, ratio)], whole.at[a], s4, k - 1, rows[k - 1]))
    for copy in copies:
        copy.wait_send()

    def emit(i, x_of, st):
        for r in range(ratio):
            cs = slice(r * width, (r + 1) * width)
            x = x_of(r)
            own_ref[i, :, cs] = x
            normed_ref[i, :, cs] = (
                (x.astype(jnp.float32) - st[:, 0:1]) * st[:, 1:2] * gain[:, cs]
            ).astype(jnp.bfloat16)

    emit(a, lambda r: gath[a * ratio + r], stat[...])
    for copy in moved:
        copy.wait()
    for k in range(1, chans):
        i = lax.rem(a + k, chans)
        emit(i, lambda r: whole[i, r], stats[i])


def layer_rows(partial, gain, chans, hids):
    tok, width = partial.shape
    size = tok // chans
    wide = gain.shape[0]
    vm = pl.BlockSpec(memory_space=pltpu.VMEM)
    dma = pltpu.SemaphoreType.DMA
    shape = jax.ShapeDtypeStruct((chans, size, wide), jnp.bfloat16)
    normed, own = pl.pallas_call(
        functools.partial(layer_kernel, chans, hids), out_shape=(shape, shape), in_specs=[vm, vm], out_specs=(vm, vm),
        scratch_shapes=[
            pltpu.VMEM((chans - 1, size, width), jnp.bfloat16), pltpu.VMEM((hids, size, width), jnp.bfloat16),
            pltpu.VMEM((size, HS), jnp.float32), pltpu.VMEM((chans, hids // chans, size, width), jnp.bfloat16),
            pltpu.VMEM((chans, size, HS), jnp.float32),
            dma((2, chans - 1)), dma((2, hids // 2 - 1)), dma((2, hids // 2)), dma((2, chans - 1)), dma((2, chans - 1))],
        compiler_params=pltpu.CompilerParams(collective_id=1, has_side_effects=True, vmem_limit_bytes=40 << 20),
        name="layer_rows",
    )(partial.reshape(chans, size, width), gain.reshape(1, wide))
    return normed.reshape(tok, wide), own.reshape(tok, wide)


def finish_kernel(chans, hids, heads, qkv, up, bias, qkv_out, hid_out, qkv_in, up_in, s1, s2, s3, s4):
    a, rows = lax.axis_index("chan"), [{"chan": lax.rem(lax.axis_index("chan") + k, chans)} for k in range(1, chans)]
    greet(rows)
    got_q = [send(qkv.at[:, lax.rem(a + k, chans)], qkv_in.at[k - 1], s1, k - 1, rows[k - 1]) for k in range(1, chans)]
    got_u = [send(up.at[lax.rem(a + k, chans)], up_in.at[k - 1], s2, k - 1, rows[k - 1]) for k in range(1, chans)]
    for copy in got_q:
        copy.wait_recv()
    for h in range(3 * heads):
        kind, hs = h // heads, slice(h % heads * HS, (h % heads + 1) * HS)
        x = qkv[kind, a, :, hs].astype(jnp.float32)
        for k in range(chans - 1):
            x = x + qkv_in[k, kind, :, hs].astype(jnp.float32)
        if h < 2 * heads:
            x = x * lax.rsqrt(jnp.mean(x * x, axis=-1, keepdims=True) + epsilon)
        qkv_out[h, a] = x.astype(jnp.bfloat16)
    put_q = [send(qkv_out.at[:, a], qkv_out.at[:, a], s3, k, peer) for k, peer in enumerate(rows)]
    for copy in got_u:
        copy.wait_recv()
    step = HS
    for n in range(up.shape[2] // step):
        cs = slice(n * step, (n + 1) * step)
        x = up[a, :, cs].astype(jnp.float32)
        for k in range(chans - 1):
            x = x + up_in[k, :, cs].astype(jnp.float32)
        x = x + bias[:, cs]
        hid_out[a, :, cs] = ((0.5 * x) * (1.0 + lax.erf(x * math.sqrt(0.5)))).astype(jnp.bfloat16)
    put_u = [send(hid_out.at[a], hid_out.at[a], s4, k, peer) for k, peer in enumerate(rows)]
    for copy in got_q + got_u:
        copy.wait_send()
    for copy in put_q + put_u:
        copy.wait()


def finish(qkv, up, bias, heads, chans, hids):
    tok, wide = qkv.shape[1:]
    size, units = tok // chans, up.shape[1]
    vm = pl.BlockSpec(memory_space=pltpu.VMEM)
    dma = pltpu.SemaphoreType.DMA
    q, u = pl.pallas_call(
        functools.partial(finish_kernel, chans, hids, heads),
        out_shape=(jax.ShapeDtypeStruct((3 * heads, chans, size, HS), jnp.bfloat16), jax.ShapeDtypeStruct((chans, size, units), jnp.bfloat16)),
        in_specs=[vm] * 3, out_specs=(vm, vm),
        scratch_shapes=[
            pltpu.VMEM((chans - 1, 3, size, wide), jnp.bfloat16), pltpu.VMEM((chans - 1, size, units), jnp.bfloat16)]
        + [dma((2, chans - 1))] * 4,
        compiler_params=pltpu.CompilerParams(collective_id=2, has_side_effects=True, vmem_limit_bytes=40 << 20),
        name="finish",
    )(qkv.reshape(3, chans, size, wide), up.reshape(chans, size, units), bias.reshape(1, units))
    return q.reshape(3, heads, tok, HS), u.reshape(tok, units)


def total_kernel(hids, term, own, out, pair, half, pieces, s1, s2, s3, s4):
    b = lax.axis_index("hid")
    chips, chip, core = hids // 2, b // 2, b % 2
    far = [{"hid": lax.rem(chip + k, chips) * 2 + core} for k in range(1, chips)]
    mate = {"hid": chip * 2 + (1 - core)}
    greet(far + [mate])
    across = send(term.at[1 - core], pair, s1, 0, mate)
    across.wait_recv()
    for i in range(chips):
        half[i] = (term[core, i].astype(jnp.float32) + pair[i].astype(jnp.float32)).astype(jnp.bfloat16)
    copies = [send(half.at[lax.rem(chip + k, chips)], pieces.at[k - 1], s2, k - 1, far[k - 1]) for k in range(1, chips)]
    value = half[chip].astype(jnp.float32)
    for k in range(chips - 1):
        copies[k].wait_recv()
        value = value + pieces[k].astype(jnp.float32)
    out[core, chip] = (value + own[core, chip].astype(jnp.float32)).astype(jnp.bfloat16)
    spread(lambda i: out.at[i % 2, i // 2], None, chips, chip, core, far, mate, s3, s4)
    across.wait_send()
    for copy in copies:
        copy.wait_send()


def total(term, own, hids):
    tok, wide = term.shape
    chips, size = hids // 2, tok // hids
    vm = pl.BlockSpec(memory_space=pltpu.VMEM)
    dma = pltpu.SemaphoreType.DMA
    out = pl.pallas_call(
        functools.partial(total_kernel, hids),
        out_shape=jax.ShapeDtypeStruct((2, chips, size, wide), jnp.bfloat16), in_specs=[vm] * 2, out_specs=vm,
        scratch_shapes=[
            pltpu.VMEM((chips, size, wide), jnp.bfloat16), pltpu.VMEM((chips, size, wide), jnp.bfloat16),
            pltpu.VMEM((chips - 1, size, wide), jnp.bfloat16),
            dma((2, 1)), dma((2, chips - 1)), dma((2, chips - 1)), dma((2, chips))],
        compiler_params=pltpu.CompilerParams(collective_id=3, has_side_effects=True, vmem_limit_bytes=40 << 20),
        name="total",
    )(term.reshape(2, chips, size, wide), own.reshape(2, chips, size, wide))
    return out.reshape(tok, wide)


def on_device(
    chans,
    hids,
    pixels,
    patch_weight,
    channel_embed,
    pool_query,
    group_mix,
    assign,
    ln_gain,
    w_qkv,
    w_up,
    b_up,
    w_out,
    w_down,
):
    tok_count = pixels.shape[1]
    width_hid = patch_weight.shape[2]
    heads_dev = width_hid // HS
    partial_value = pool(pixels, patch_weight, channel_embed, pool_query, group_mix, assign)
    normed_input, own_cols = layer_rows(partial_value, ln_gain, chans, hids)
    qkv_part = jnp.einsum("td,dke->kte", normed_input, w_qkv, preferred_element_type=jnp.float32)
    up_part = jnp.dot(normed_input, w_up, preferred_element_type=jnp.float32)
    qkv_rows, hidden = finish(
        qkv_part.astype(jnp.bfloat16), up_part.astype(jnp.bfloat16), b_up, heads_dev, chans, hids
    )
    images = tok_count // PATCHES
    queries, keys, values = qkv_rows.reshape(3, heads_dev, images, PATCHES, HS)
    scores = jnp.einsum("hbqe,hbke->hbqk", queries, keys, preferred_element_type=jnp.float32) * (
        2.0 / math.sqrt(HS)
    )
    expo = jnp.exp(scores)
    probs = (expo / jnp.sum(expo, axis=-1, keepdims=True)).astype(jnp.bfloat16)
    attended = jnp.einsum("hbqk,hbke->bqhe", probs, values, preferred_element_type=jnp.float32)
    attended = attended.astype(jnp.bfloat16).reshape(tok_count, width_hid)
    term = jnp.dot(attended, w_out, preferred_element_type=jnp.float32) + jnp.dot(
        hidden, w_down, preferred_element_type=jnp.float32
    )
    term = term.astype(jnp.bfloat16)
    if tok_count % (16 * hids) == 0:
        return total(term, own_cols, hids)
    mixed = lax.psum(term, "hid").astype(jnp.float32)
    return (own_cols.astype(jnp.float32) + mixed).astype(jnp.bfloat16)


def solution(mesh):
    in_specs = (
        P("chan", None, None),
        P("chan", None, "hid"),
        P("chan", "hid"),
        P("chan", "hid"),
        P("chan", "hid"),
        P("chan"),
        P("chan"),
        P("chan", None, "hid"),
        P("chan", "hid"),
        P("hid"),
        P("hid", "chan"),
        P("hid", "chan"),
    )
    out_specs = P(None, "chan")
    chans, hids = mesh.shape["chan"], mesh.shape["hid"]
    return jax.shard_map(
        functools.partial(on_device, chans, hids), mesh=mesh, in_specs=in_specs, out_specs=out_specs, check_vma=False
    )
```

time: 396 us -> 250 us (0.63)
  waiting for transfers between devices: 196 us -> 0 us
  Pallas kernels: 106 us -> 219 us
  blocking collectives: 31.2 us -> 0 us
  between operations: 13.7 us -> 0.19 us
  other arithmetic: 15.4 us -> 1.93 us
  matrix products: 25.6 us -> 15.3 us
  local copies, waits for them, and re-layouts: 5.74 us -> 10.6 us
    pallas_call x0 -> x3, Pallas kernels: none -> 119 us  [the longest x1 62.8 us: finish(): pl.pallas_call(functools.partial(finish_kernel, chans, hids, heads), out_...]
    psum x2 -> x0, waiting for transfers between devices: 104 us -> none  [the longest x1 57.2 us: on_device(): mixed = lax.psum(term.astype(jnp.bfloat16), 'hid').astype(jnp.float32)]
    reduce_scatter x2 -> x0, waiting for transfers between devices: 51.6 us -> none  [the longest x1 28 us: on_device(): lax.psum_scatter(qkv_part.astype(jnp.bfloat16), 'chan', scatter_dimension...]
    all_gather x2 -> x0, waiting for transfers between devices: 39.8 us -> none  [the longest x1 39.8 us: on_device(): gathered = lax.all_gather(layer_sum, 'hid', axis=1, tiled=True)]
    all_gather x3 -> x0, blocking collectives: 31.2 us -> none  [the longest x1 11.9 us: on_device(): lax.all_gather(query_share, 'chan', axis=0, tiled=True)]
    unnamed x10 -> x17, local copies, waits for them, and re-layouts: 0.02 us -> 7.13 us
    convert_element_type x4 -> x0, other arithmetic: 6.66 us -> none  [the longest x1 3.46 us: finish_rows(): jax.nn.gelu(up_rows + b_up, approximate=False).astype(jnp.bfloat16)]
    pallas_call x1, Pallas kernels: 106 us -> 99.9 us  [pool(): pl.pallas_call(functools.partial(pool_kernel, size), grid_spec=spec, out_...]
  transfers between devices with their start and end apart: 6 -> 0, of which waited for: 5 -> 0; matrix products, arithmetic and copies ran while one was open for 5% -> 0% of each run, Pallas kernels for 0% -> 0%
where the time goes in v2:
time: 250 us; the launch traced here: 247 us
  Pallas kernels  219 us (88%)
  matrix products  15.3 us (6%)
  local copies, waits for them, and re-layouts  10.6 us (4%)
    pallas_call x1, Pallas kernels, pool(): pl.pallas_call(functools.partial(pool_kernel, size), grid_spec=spec, out_...  99.9 us
    pallas_call x1, Pallas kernels, finish(): pl.pallas_call(functools.partial(finish_kernel, chans, hids, heads), out_...  62.8 us
    pallas_call x1, Pallas kernels, layer_rows(): pl.pallas_call(functools.partial(layer_kernel, chans, hids), out_shape=(s...  34 us
    pallas_call x1, Pallas kernels, total(): pl.pallas_call(functools.partial(total_kernel, hids), out_shape=jax.Shape...  21.9 us
    unnamed x17, local copies, waits for them, and re-layouts  7.13 us

profile of v2, /device:TPU:0, one launch (start us, length us, event | category | flops | bytes accessed | tf_op | source)
XLA Modules:
  0.0 246.6 jit_solution(7938500509415753155)
XLA Ops:
  0.0 0.8 iota_add_fusion
  0.8 0.2 convert_reduce_fusion
  1.0 0.1 select_reduce_fusion.order_ref
  1.1 0.7 reshape.92.gain
  1.8 0.8 reshape.107.mix_ref
  2.6 0.8 reshape.86.query_ref
  3.3 0.7 convert_multiply_fusion
  4.1 0.1 reduce_sum.38
  4.2 1.1 reshape.105.emb_ref
  5.3 4.6 %copy-done.1 = bf16[96,256,256]{2,1,0:T(8,128)(2,1)S(1)} copy-done((bf16[96,256,256]{2,1,0:T(8,128)(2,1)S(1)}, bf16[96,256,256]{2,1,0:T(8,128)(2,1)}, u32[]{:S(2)}) %copy-start.1) | copy-done | bytes 12582936
  9.9 99.9 %pool.1 = bf16[256,768]{1,0:T(8,128)(2,1)S(1)} custom-call(s32[96]{0:T(128)S(1)} %select_reduce_fusion.order_ref, bf16[96,256,256]{2,1,0:T(8,128)(2,1)S(1)} %copy-done.1, bf16[96,256,768]{2,1,0:T(8,128)(2,1)} %pw_ref.1, f32[96,1,768]{2,1,0:T(1,128)S(1)} %reshape.105.emb_ref, f32[12,1,768]{2,1,0:T(1,128)S(1)} %reshape.86.query_ref, ...), custom_call_target="tpu_custom_call" | custom-call | tf_op jit(solution)/shard_map/pool/pallas_call | solution.py:98
  109.8 34.0 %layer_rows.1 = (bf16[4,64,1536]{2,1,0:T(8,128)(2,1)S(1)}, bf16[4,64,1536]{2,1,0:T(8,128)(2,1)S(1)}) custom-call(bf16[4,64,768]{2,1,0:T(8,128)(2,1)S(1)} %bitcast.35, f32[1,1536]{1,0:T(1,128)S(1)} %reshape.92.gain), custom_call_target="tpu_custom_call" | custom-call | tf_op jit(solution)/shard_map/layer_rows/pallas_call | solution.py:205
  143.9 0.0 slice-start
  143.9 2.0 convolution_convert_fusion.1
  145.9 1.6 copy-done.3
  147.5 2.6 %convolution_convert_fusion = bf16[256,3072]{1,0:T(8,128)(2,1)S(1)} fusion(bf16[256,1536]{1,0:T(8,128)(2,1)S(1)} %bitcast.42, bf16[1536,3072]{1,0:T(8,128)(2,1)S(1)} %copy-done.3), kind=kOutput, calls=%fused_computation | convolution fusion | flops 2416705536 | bytes 11796480 | tf_op jit(solution)/shard_map/dot_general | solution.py:331
  150.2 62.8 %finish.1 = (bf16[18,4,64,128]{3,2,1,0:T(8,128)(2,1)S(1)}, bf16[4,64,3072]{2,1,0:T(8,128)(2,1)S(1)}) custom-call(bf16[3,4,64,768]{3,2,1,0:T(8,128)(2,1)S(1)} %bitcast.37, bf16[4,64,3072]{2,1,0:T(8,128)(2,1)S(1)} %bitcast.36, f32[1,3072]{1,0:T(1,128)S(1)} %bitcast.39), custom_call_target="tpu_custom_call" | custom-call | tf_op jit(solution)/shard_map/finish/pallas_call | solution.py:256
  213.0 3.8 %fusion.4 = f32[256,1536]{1,0:T(8,128)} fusion(bf16[256,3072]{1,0:T(8,128)(2,1)S(1)} %bitcast.40, bf16[3072,1536]{1,0:T(8,128)(2,1)S(1)} %bitcast.48), kind=kOutput, calls=%fused_computation.15 | convolution fusion | flops 2415919104 | bytes 12582912 | tf_op jit(solution)/shard_map/dot_general | solution.py:344
  216.8 0.1 fusion.3
  216.9 1.5 multiply_exponential_fusion
  218.4 3.0 %convolution_convert_fusion.2 = bf16[6,128,256]{2,1,0:T(8,128)(2,1)} fusion(bf16[6,256,128]{2,1,0:T(8,128)(2,1)S(1)} %bitcast.45, f32[6,256,256]{1,2,0:T(8,128)} %multiply_exponential_fusion), kind=kOutput, calls=%fused_computation.6 | convolution fusion | flops 101648128 | bytes 2359296 | tf_op jit(solution)/shard_map/hbqk,hbke->bqhe/dot_general | solution.py:342
  221.5 2.3 fusion
  223.8 21.9 %total.1 = bf16[2,4,32,1536]{3,2,1,0:T(8,128)(2,1)S(1)} custom-call(bf16[2,4,32,1536]{3,2,1,0:T(8,128)(2,1)S(1)} %bitcast.33, bf16[2,4,32,1536]{3,2,1,0:T(8,128)(2,1)S(1)} %bitcast.38), custom_call_target="tpu_custom_call" | custom-call | tf_op jit(solution)/shard_map/total/pallas_call | solution.py:296
  245.7 0.9 copy.20
  (18 shorter events, 0.1 us)
Async XLA Ops:
  0.0 221.5 %copy-start = (bf16[768,1536]{1,0:T(8,128)(2,1)S(1)}, bf16[768,1536]{1,0:T(8,128)(2,1)}, u32[]{:S(2)}) copy-start(bf16[768,1536]{1,0:T(8,128)(2,1)} %param.22) | copy-start | bytes 7077892
  5.3 4.6 %copy-start.1 = (bf16[96,256,256]{2,1,0:T(8,128)(2,1)S(1)}, bf16[96,256,256]{2,1,0:T(8,128)(2,1)}, u32[]{:S(2)}) copy-start(bf16[96,256,256]{2,1,0:T(8,128)(2,1)} %pix_ref.1) | copy-start | bytes 37748740
  9.9 134.0 %copy-start.4 = (bf16[1536,3,768]{2,0,1:T(8,128)(2,1)S(1)}, bf16[1536,3,768]{2,0,1:T(8,128)(2,1)}, u32[]{:S(2)}) copy-start(bf16[1536,3,768]{2,0,1:T(8,128)(2,1)} %param.19) | copy-start | bytes 21233668
  143.8 3.7 %copy-start.3 = (bf16[1536,3072]{1,0:T(8,128)(2,1)S(1)}, bf16[1536,3072]{1,0:T(8,128)(2,1)}, u32[]{:S(2)}) copy-start(bf16[1536,3072]{1,0:T(8,128)(2,1)} %param.20) | copy-start | bytes 28311556
  143.9 69.1 %slice-start = ((s8[9437184]{0:T(1024)(128)(4,1)}), s8[4194304]{0:T(1024)(128)(4,1)S(1)}, s32[]{:S(2)}) async-start(s8[9437184]{0:T(1024)(128)(4,1)} %bitcast.47), calls=%async_computation | async-start | bytes 8388608
  143.9 69.1 %slice-start.1 = ((s8[9437184]{0:T(1024)(128)(4,1)}), s8[4194304]{0:T(1024)(128)(4,1)S(1)}, s32[]{:S(2)}) async-start(s8[9437184]{0:T(1024)(128)(4,1)} %bitcast.47), calls=%async_computation.1 | async-start | bytes 8388608
  147.5 2.6 %copy-start.2 = (f32[3072]{0:T(1024)S(1)}, f32[3072]{0:T(1024)}, u32[]{:S(2)}) copy-start(f32[3072]{0:T(1024)} %param.21) | copy-start | bytes 36868
  147.5 65.4 %slice-start.2 = ((s8[9437184]{0:T(1024)(128)(4,1)}), s8[1048576]{0:T(1024)(128)(4,1)S(1)}, s32[]{:S(2)}) async-start(s8[9437184]{0:T(1024)(128)(4,1)} %bitcast.47), calls=%async_computation.2 | async-start | bytes 2097152
